TPU v7x, 128 devices: a whole 4x4x4 slice. The times are simulated.
128 devices in a mesh: board: 32 (over x, y, core), hand: 4 (over z).
Axes of the slice: x: 4, y: 4, z: 4, core: 2. Of those that a mesh axis runs over, the one named last changes fastest.
Arguments:
- reach_pre: float32 [1408], P(('board', 'hand')), may hold values from 0.05 to 1
- strategy: bfloat16 [256, 128, 1408], P('board', None, 'hand'), may hold values from 0 to 1
- ranks: int32 [256, 8, 1408], P('board'), may hold values from 0 to 94
- boards: int32 [256, 8, 5], P('board'), may hold values from 0 to 51, as said below
- river_live: int32 [256], P('board'), may hold values from 1 to 8, as said below
- iso_weight: int32 [256], P('board'), may hold values from 1 to 24
- pot: float32 [128], replicated, may hold values from 2 to 24
- line_act: int32 [128], replicated, may hold values from 0 to 2
Outputs:
- preflop_value: float32 [1408], P('hand')
Inputs may be any that keep to these rules, and one draw needn't show every extreme that they name: `boards`: the five cards of a runout are distinct; all runouts of a flop share their first three cards. `river_live`: in every draw some flop has all 8 runouts live.
All inputs are finite; a program needn't handle non-finite values.
Results may differ from a plain program's by a relative error of at most 0.0003.
Values may be sent and summed in bfloat16 or wider, within the bound.
A program may use at most 64 MiB of HBM per device.

v0:
```python
import jax
import jax.numpy as jnp
import numpy as np
from jax import lax
from jax.sharding import PartitionSpec as P

HANDS = 1326
HPAD = 1408
ACTS = 3


def card_tables():
    first_card, second_card = np.triu_indices(52, 1)
    padding = HPAD - HANDS
    first_card = np.concatenate([first_card, np.full(padding, 52)]).astype(np.int32)
    second_card = np.concatenate([second_card, np.full(padding, 53)]).astype(np.int32)
    alive_mask = np.concatenate([np.ones(HANDS), np.zeros(padding)]).astype(np.float32)
    return (jnp.asarray(first_card), jnp.asarray(second_card), jnp.asarray(alive_mask))


def unblocked(first_rows, second_rows, first_cols, second_cols):
    clear = (first_rows[:, None] != first_cols[None, :]) & (
        first_rows[:, None] != second_cols[None, :]
    )
    clear = (
        clear
        & (second_rows[:, None] != first_cols[None, :])
        & (second_rows[:, None] != second_cols[None, :])
    )
    return clear.astype(jnp.float32)


def live_hands(first_card, second_card, alive_mask, board_cards):
    clear = jnp.all(
        (first_card[:, None] != board_cards[None, :])
        & (second_card[:, None] != board_cards[None, :]),
        axis=1,
    )
    return alive_mask * clear.astype(jnp.float32)


def showdown(rank_rows, rank_cols, live_rows, live_cols, blocking):
    signed = jnp.sign(rank_rows[:, None] - rank_cols[None, :]).astype(jnp.float32)
    return (signed * blocking.astype(jnp.float32) * live_rows[:, None] * live_cols[None, :]).astype(
        jnp.bfloat16
    )


def runout_sum(
    ranks_flop, boards_flop, count_flop, tables, row_span, col_span, blocking, reach_flop
):
    first_card, second_card, alive_mask = tables
    row_start, row_len = row_span
    col_start, col_len = col_span

    def add_runout(runout, acc, factor):
        rank_now = ranks_flop[runout]
        live_now = live_hands(first_card, second_card, alive_mask, boards_flop[runout])
        matrix = showdown(
            lax.dynamic_slice_in_dim(rank_now, row_start, row_len),
            rank_now,
            lax.dynamic_slice_in_dim(live_now, row_start, row_len),
            lax.dynamic_slice_in_dim(live_now, col_start, col_len),
            blocking,
        )
        values = lax.dot_general(
            matrix, reach_flop, (((1,), (1,)), ((), ())), preferred_element_type=jnp.float32
        )
        return acc + values * factor

    empty = jnp.zeros((row_len, reach_flop.shape[0]), jnp.float32)

    def every_step(runout, acc):
        return add_runout(runout, acc, (runout < count_flop).astype(jnp.float32))

    return lax.fori_loop(0, ranks_flop.shape[0], every_step, empty)


def body(reach_pre, strategy, ranks, boards, river_live, iso_weight, pot, line_act):
    tables = card_tables()
    first_card, second_card, alive_mask = tables
    full_reach = lax.all_gather(reach_pre, ("board", "hand"), axis=0, tiled=True)
    local_weight = jnp.sum(iso_weight.astype(jnp.float32))
    weight_total = lax.psum(local_weight, "board")
    total_reach = jnp.sum(full_reach * alive_mask)
    hand_rows = strategy.shape[2]
    slots = full_reach.shape[0]
    row_start = lax.axis_index("hand") * hand_rows
    own_first = lax.dynamic_slice_in_dim(first_card, row_start, hand_rows)
    own_second = lax.dynamic_slice_in_dim(second_card, row_start, hand_rows)
    own_reach = lax.dynamic_slice_in_dim(full_reach, row_start, hand_rows)
    line_reach = (own_reach[None, None, :] * strategy.astype(jnp.float32) / total_reach).astype(
        jnp.bfloat16
    )
    onehot = (line_act[:, None] == jnp.arange(ACTS, dtype=jnp.int32)[None, :]).astype(jnp.float32)
    flop_ids = jnp.arange(strategy.shape[0], dtype=jnp.int32)
    every_reach = lax.all_gather(line_reach, "hand", axis=2, tiled=True)
    blocking = unblocked(own_first, own_second, first_card, second_card).astype(jnp.bfloat16)

    def own_rows(flop_index):
        return runout_sum(
            ranks[flop_index],
            boards[flop_index],
            river_live[flop_index],
            tables,
            (row_start, hand_rows),
            (0, slots),
            blocking,
            every_reach[flop_index],
        )

    acc = lax.map(own_rows, flop_ids)
    line_values = acc * pot[None, None, :] / river_live.astype(jnp.float32)[:, None, None]
    group_values = jnp.dot(
        line_values, onehot, precision=lax.Precision.HIGHEST, preferred_element_type=jnp.float32
    )
    best = jnp.max(group_values, axis=2)
    partial_values = jnp.sum(iso_weight.astype(jnp.float32)[:, None] * best, axis=0)
    summed = lax.psum(partial_values, "board")
    return summed / weight_total


def solution(mesh):
    in_specs = (
        P(("board", "hand")),
        P("board", None, "hand"),
        P("board", None, None),
        P("board", None, None),
        P("board"),
        P("board"),
        P(),
        P(),
    )
    out_specs = P("hand")
    return jax.shard_map(body, mesh=mesh, in_specs=in_specs, out_specs=out_specs, check_vma=False)
```

profile of v0, /device:TPU:1, one launch (start us, length us, event | category | flops | bytes accessed | tf_op | source)
XLA Modules:
  0.0 367.4 jit_solution(5847999569311250122)
XLA Ops:
  7.5 68.7 %all-reduce = f32[1408]{0:T(1024)S(1)} all-reduce(f32[1408]{0:T(1024)S(1)} %dynamic-update-slice), channel_id=1, replica_groups=mesh['board'=32,'hand'=4] {'board','hand'}, use_global_device_ids=true, to_apply=%add | all-reduce | flops 1408 | bytes 11264
  76.2 1.3 multiply_reduce_fusion.1
  77.5 3.0 divide_convert_fusion
  81.4 33.1 %all-gather.2.cloned.1.call-done = bf16[8,128,1408]{1,0,2:T(8,128)(2,1)} async-done(((bf16[8,128,352]{1,0,2:T(8,128)(2,1)}), bf16[8,128,1408]{1,0,2:T(8,128)(2,1)}) %all-gather.2.cloned.1.call-update) | async-done | bytes 2883600 | tf_op jit(solution)/shard_map/all_gather | solution.py:97
  114.5 4.8 %copy.19 = bf16[8,128,1408]{2,1,0:T(8,128)(2,1)} copy(bf16[8,128,1408]{1,0,2:T(8,128)(2,1)} %all-gather.2.cloned.1.call-done) | data formatting | bytes 5767168
  119.4 175.5 %while.50 = (s32[]{:T(128)}, f32[8,352,128]{2,1,0:T(8,128)S(1)}, s32[8]{0:T(128)S(1)}, s32[8]{0:T(128)S(1)}, s32[8,8,1408]{2,1,0:T(8,128)}, /*index=5*/s32[8,8,5...) while((s32[]{:T(128)}, f32[8,352,128]{2,1,0:T(8,128)S(1)}, ...), condition=%wide.region_5.6_spmd.clone.clone, body=%wide.region_1.5_spmd.sunk.clone.clone.sunk | while | flops 135466512 | bytes 3946544 | solution.py:112
  122.1 1.0 dynamic-slice_bitcast_fusion.7
  126.0 15.2 %while.51 = (s32[]{:T(128)}, f32[352,128]{1,0:T(8,128)S(1)}, s32[8,1408]{1,0:T(8,128)S(1)}, s32[]{:T(128)}, bf16[352,1408]{1,0:T(8,128)(2,1)S(1)}, /*index=5*/s3...) while((s32[]{:T(128)}, f32[352,128]{1,0:T(8,128)S(1)}, ...), condition=%wide.region_4.4_spmd.clone.clone, body=%wide.region_2.0_spmd.sunk.clone.clone.sunk | while | flops 131005960 | bytes 1768713 | solution.py:76
  127.0 0.9 fusion.17
  132.8 0.9 fusion.17
  138.5 0.9 fusion.17
  144.0 1.0 dynamic-slice_bitcast_fusion.7
  148.0 15.2 %while.51 = (s32[]{:T(128)}, f32[352,128]{1,0:T(8,128)S(1)}, s32[8,1408]{1,0:T(8,128)S(1)}, s32[]{:T(128)}, bf16[352,1408]{1,0:T(8,128)(2,1)S(1)}, /*index=5*/s3...) while((s32[]{:T(128)}, f32[352,128]{1,0:T(8,128)S(1)}, ...), condition=%wide.region_4.4_spmd.clone.clone, body=%wide.region_2.0_spmd.sunk.clone.clone.sunk | while | flops 131005960 | bytes 1768713 | solution.py:76
  149.0 0.9 fusion.17
  165.9 1.0 dynamic-slice_bitcast_fusion.7
  169.9 15.2 %while.51 = (s32[]{:T(128)}, f32[352,128]{1,0:T(8,128)S(1)}, s32[8,1408]{1,0:T(8,128)S(1)}, s32[]{:T(128)}, bf16[352,1408]{1,0:T(8,128)(2,1)S(1)}, /*index=5*/s3...) while((s32[]{:T(128)}, f32[352,128]{1,0:T(8,128)S(1)}, ...), condition=%wide.region_4.4_spmd.clone.clone, body=%wide.region_2.0_spmd.sunk.clone.clone.sunk | while | flops 131005960 | bytes 1768713 | solution.py:76
  170.9 0.9 fusion.17
  172.8 0.9 fusion.17
  176.6 0.9 fusion.17
  187.9 1.0 dynamic-slice_bitcast_fusion.7
  191.8 15.2 %while.51 = (s32[]{:T(128)}, f32[352,128]{1,0:T(8,128)S(1)}, s32[8,1408]{1,0:T(8,128)S(1)}, s32[]{:T(128)}, bf16[352,1408]{1,0:T(8,128)(2,1)S(1)}, /*index=5*/s3...) while((s32[]{:T(128)}, f32[352,128]{1,0:T(8,128)S(1)}, ...), condition=%wide.region_4.4_spmd.clone.clone, body=%wide.region_2.0_spmd.sunk.clone.clone.sunk | while | flops 131005960 | bytes 1768713 | solution.py:76
  209.8 1.0 dynamic-slice_bitcast_fusion.7
  213.8 15.2 %while.51 = (s32[]{:T(128)}, f32[352,128]{1,0:T(8,128)S(1)}, s32[8,1408]{1,0:T(8,128)S(1)}, s32[]{:T(128)}, bf16[352,1408]{1,0:T(8,128)(2,1)S(1)}, /*index=5*/s3...) while((s32[]{:T(128)}, f32[352,128]{1,0:T(8,128)S(1)}, ...), condition=%wide.region_4.4_spmd.clone.clone, body=%wide.region_2.0_spmd.sunk.clone.clone.sunk | while | flops 131005960 | bytes 1768713 | solution.py:76
  231.7 1.0 dynamic-slice_bitcast_fusion.7
  235.7 15.2 %while.51 = (s32[]{:T(128)}, f32[352,128]{1,0:T(8,128)S(1)}, s32[8,1408]{1,0:T(8,128)S(1)}, s32[]{:T(128)}, bf16[352,1408]{1,0:T(8,128)(2,1)S(1)}, /*index=5*/s3...) while((s32[]{:T(128)}, f32[352,128]{1,0:T(8,128)S(1)}, ...), condition=%wide.region_4.4_spmd.clone.clone, body=%wide.region_2.0_spmd.sunk.clone.clone.sunk | while | flops 131005960 | bytes 1768713 | solution.py:76
  253.7 1.0 dynamic-slice_bitcast_fusion.7
  257.6 15.2 %while.51 = (s32[]{:T(128)}, f32[352,128]{1,0:T(8,128)S(1)}, s32[8,1408]{1,0:T(8,128)S(1)}, s32[]{:T(128)}, bf16[352,1408]{1,0:T(8,128)(2,1)S(1)}, /*index=5*/s3...) while((s32[]{:T(128)}, f32[352,128]{1,0:T(8,128)S(1)}, ...), condition=%wide.region_4.4_spmd.clone.clone, body=%wide.region_2.0_spmd.sunk.clone.clone.sunk | while | flops 131005960 | bytes 1768713 | solution.py:76
  275.6 1.0 dynamic-slice_bitcast_fusion.7
  279.6 15.2 %while.51 = (s32[]{:T(128)}, f32[352,128]{1,0:T(8,128)S(1)}, s32[8,1408]{1,0:T(8,128)S(1)}, s32[]{:T(128)}, bf16[352,1408]{1,0:T(8,128)(2,1)S(1)}, /*index=5*/s3...) while((s32[]{:T(128)}, f32[352,128]{1,0:T(8,128)S(1)}, ...), condition=%wide.region_4.4_spmd.clone.clone, body=%wide.region_2.0_spmd.sunk.clone.clone.sunk | while | flops 131005960 | bytes 1768713 | solution.py:76
  294.9 1.1 fusion.7
  296.1 63.4 %all-reduce.1 = (f32[352]{0:T(512)S(1)}, f32[]{:T(128)}) all-reduce(f32[352]{0:T(512)S(1)} %multiply_reduce_fusion, f32[]{:T(128)} %convert_reduce_fusion), channel_id=1, replica_groups=mesh['board'=32,'hand'=4] {'board'}, use_global_device_ids=true, to_apply=%region_8.9 | all-reduce | flops 353 | bytes 2824 | tf_op jit(solution)/shard_map/psum | solution.py:119
  359.4 1.1 broadcast_divide_fusion
  (532 shorter events, 100.9 us)
Async XLA Ops:
  6.5 74.1 %copy-start = (s32[1408]{0:T(1024)S(1)}, s32[1408]{0:T(1024)}, u32[]{:S(2)}) copy-start(s32[1408]{0:T(1024)} %constant.188.clone) | copy-start | bytes 16900
  6.5 74.2 %copy-start.1 = (s32[1408]{0:T(1024)S(1)}, s32[1408]{0:T(1024)}, u32[]{:S(2)}) copy-start(s32[1408]{0:T(1024)} %constant.189.clone) | copy-start | bytes 16900
  6.5 74.2 %copy-start.4 = (s32[8]{0:T(128)S(1)}, s32[8]{0:T(128)}, u32[]{:S(2)}) copy-start(s32[8]{0:T(128)} %param.19) | copy-start | bytes 100
  6.5 74.2 %copy-start.3 = (s32[8]{0:T(128)S(1)}, s32[8]{0:T(128)}, u32[]{:S(2)}) copy-start(s32[8]{0:T(128)} %param.20) | copy-start | bytes 100
  6.5 108.0 %all-gather.2.cloned.1.call-start = ((), (), s32[]{:S(2)}) async-start(), calls=%async_computation | async-start | bytes 3604480 | tf_op jit(solution)/shard_map/all_gather | solution.py:97
  81.4 38.0 %copy-start.2 = (f32[1408]{0:T(1024)S(1)}, f32[1408]{0:T(1024)}, u32[]{:S(2)}) copy-start(f32[1408]{0:T(1024)} %constant.190.clone) | copy-start | bytes 16900
  119.4 175.5 %copy-start.5 = (f32[128]{0:T(128)S(1)}, f32[128]{0:T(128)}, u32[]{:S(2)}) copy-start(f32[128]{0:T(128)} %param.21) | copy-start | bytes 1540
  119.4 175.5 %copy-start.6 = (s32[128]{0:T(128)S(1)}, s32[128]{0:T(128)}, u32[]{:S(2)}) copy-start(s32[128]{0:T(128)} %param.22) | copy-start | bytes 1540
Sparse Core Ops, SparseCore 0:
  80.7 33.7 all-gather.1
where the time goes:
time: 373 us; the launch traced here: 367 us
  blocking collectives  132 us (35%)
  loops' own time  62.2 us (17%)
  matrix products  57.1 us (15%)
  local copies, waits for them, and re-layouts  50.9 us (14%)
  waiting for transfers between devices  33.1 us (9%)
  other arithmetic  18.5 us (5%)
  between operations  13.5 us (4%)
    unnamed x1, blocking collectives  68.7 us
    psum x1, blocking collectives, body(): summed = lax.psum(partial_values, 'board')  63.4 us
    dot_general x64, matrix products, add_runout(): lax.dot_general(matrix, reach_flop, (((1,), (1,)), ((), ())), preferred_e...  56 us
    another operation x8, loops' own time, runout_sum(): return lax.fori_loop(0, ranks_flop.shape[0], every_step, empty)  45.6 us
    all_gather x1, waiting for transfers between devices, body(): every_reach = lax.all_gather(line_reach, 'hand', axis=2, tiled=True)  33.1 us
    another operation x1, loops' own time, body(): acc = lax.map(own_rows, flop_ids)  16.6 us
    squeeze x8, local copies, waits for them, and re-layouts, own_rows(): every_reach[flop_index]  8.15 us
  transfers between devices with their start and end apart: 1, of which 1 were waited for; matrix products, arithmetic and copies ran while one was open for 0% of the time, Pallas kernels for 0%

commit v1 on v0

v1 whole, which is shorter than its diff:
```python
import functools

import jax
import jax.numpy as jnp
import numpy as np
from jax import lax
from jax.experimental import pallas as pl
from jax.experimental.pallas import tpu as pltpu
from jax.sharding import PartitionSpec as P

HANDS = 1326
HPAD = 1408
RIV = 8
LINES = 128
ACTS = 3
NF = 8
OWN = 352
OPAD = 384
CHUNK = 11
DEAD = 128.0
XS, YS, CS, ZS = 4, 4, 2, 4
NB = XS * YS * CS
PARTS = 3
ROWS = PARTS * ACTS * NF
RPAD = 80
f32, bf16 = jnp.float32, jnp.bfloat16


def card_rows():
    first, second = np.triu_indices(52, 1)
    padding = HPAD - HANDS
    rows = np.zeros((8, HPAD), np.float32)
    rows[0] = np.concatenate([first, np.full(padding, 52)])
    rows[1] = np.concatenate([second, np.full(padding, 53)])
    rows[2] = np.arange(HPAD) < HANDS
    return rows


def pieces(value):
    high = value.astype(bf16)
    rest = value - high.astype(f32)
    middle = rest.astype(bf16)
    low = (rest - middle.astype(f32)).astype(bf16)
    return high, middle, low


def kernel(
    reach_hbm, strategy_hbm, ranks_hbm, boards_hbm, pot_hbm, act_hbm, cards_hbm, live_smem, iso_smem,
    out_ref,
    reach_in, strat, ranks, boards, pot, act, cards,
    rk, rows_b, cols_b, dead_j, block, mat, sel, pick, wslot, wall, rhs, gathered, final,
    load_sem, s1, r1, s2, r2, s3, r3, s4, r4, s5, r5,
):
    board, hand = lax.axis_index("board"), lax.axis_index("hand")
    x, y, core = board // (YS * CS), (board // CS) % YS, board % CS

    def board_of(xx, yy, cc):
        return (xx * YS + yy) * CS + cc

    near = [(dz, dc) for dz in range(ZS) for dc in range(CS) if dz or dc]

    barrier = pltpu.get_barrier_semaphore()

    def greet(b, h):
        pl.semaphore_signal(barrier, inc=1, device_id=(b, h), device_id_type=pl.DeviceIdType.MESH)

    for dz, dc in near:
        greet(board_of(x, y, (core + dc) % CS), (hand + dz) % ZS)
    for k in range(1, YS):
        greet(board_of(x, (y + k) % YS, core), hand)
    for k in range(1, XS):
        greet(board_of((x + k) % XS, y, core), hand)

    loads = [
        pltpu.make_async_copy(a, b, load_sem.at[i])
        for i, (a, b) in enumerate(
            [(reach_hbm, reach_in), (cards_hbm, cards), (boards_hbm, boards), (ranks_hbm, ranks),
             (pot_hbm, pot), (act_hbm, act), (strategy_hbm, strat)]
        )
    ]
    for c in loads:
        c.start()
    loads[0].wait()
    mine = board * ZS + hand
    gathered[pl.ds(mine, 1), 0:1, 0:CHUNK] = reach_in[...].reshape(1, 1, CHUNK)
    for c in loads[1:6]:
        c.wait()

    c1, c2, alive = cards[0:1, :], cards[1:2, :], cards[2:3, :]
    runout = lax.broadcasted_iota(jnp.int32, (RIV, 1), 0)
    for f in range(NF):
        cols = boards[f].astype(f32)
        dead = jnp.broadcast_to(alive < 0.5, (RIV, HPAD))
        for k in range(5):
            card = cols[:, k : k + 1]
            dead = dead | (c1 == card) | (c2 == card)
        dead = dead | (runout >= live_smem[f])
        here = jnp.where(dead, DEAD, ranks[f].astype(f32))
        rk[RIV * f : RIV * (f + 1), :] = here
        rk[64 + f : 65 + f, :] = jnp.sum(dead.astype(f32), axis=0, keepdims=True)
    rk[72:74, :] = cards[0:2, :]
    rk[74:80, :] = jnp.zeros((6, HPAD), f32)

    own = rk[:, 0:OPAD]
    for z in range(1, ZS):
        if z < ZS - 1:
            part = rk[:, OWN * z : OWN * z + OPAD]
        else:
            part = jnp.concatenate([rk[:, OWN * z :], jnp.zeros((80, OPAD - OWN), f32)], axis=1)
        own = jnp.where(hand == z, part, own)
    own = jnp.concatenate([own, jnp.zeros((48, OPAD), f32)], axis=0)
    columns = own.T[0:OWN, :]
    for q in range(74):
        cols_b[q] = jnp.broadcast_to(columns[:, q : q + 1], (OWN, 128)).astype(bf16)
    for q in range(74):
        rows_b[q] = jnp.broadcast_to(rk[q : q + 1, :], (16, HPAD)).astype(bf16)

    def spread(row):
        return jnp.broadcast_to(row[None], (OWN // 16, 16, 128)).reshape(OWN, 128)

    one = jnp.ones((), bf16)

    def tile_of_block(t, carry):
        at = pl.ds(pl.multiple_of(t * 128, 128), 128)
        a1, a2 = cols_b[72], cols_b[73]
        b1, b2 = spread(rows_b[72, :, at]), spread(rows_b[73, :, at])
        product = ((a1 - b1) * (a1 - b2)) * ((a2 - b1) * (a2 - b2))
        block[:, at] = jnp.minimum(jnp.abs(product), one)
        return carry

    lax.fori_loop(0, HPAD // 128, tile_of_block, 0)

    def build(lo, hi):
        def step(i, carry):
            f, t = i // (HPAD // 128), i % (HPAD // 128)
            at = pl.ds(pl.multiple_of(t * 128, 128), 128)
            acc = spread(rows_b[64 + f, :, at]) - cols_b[64 + f]
            for r in range(RIV):
                gap = cols_b[RIV * f + r] - spread(rows_b[RIV * f + r, :, at])
                acc = acc + jnp.maximum(jnp.minimum(gap, one), -one)
            mat[:, pl.ds(pl.multiple_of(f * HPAD + t * 128, 128), 128)] = acc * block[:, at]
            return carry

        lax.fori_loop(lo * (HPAD // 128), hi * (HPAD // 128), step, 0)

    flop_of_row = lax.broadcasted_iota(jnp.int32, (NF, 128), 0)
    pot_row, act_row = pot[...].reshape(1, LINES), act[...].reshape(1, LINES)
    weights = [pieces(jnp.where(act_row == a, pot_row, 0.0)) for a in range(ACTS)]
    for f in range(NF):
        groups = [
            jnp.where(flop_of_row == f, jnp.broadcast_to(weights[a][p].astype(f32), (NF, LINES)), 0.0)
            for p in range(PARTS) for a in range(ACTS)
        ] + [jnp.zeros((NF, LINES), f32)]
        sel[:, LINES * f : LINES * (f + 1)] = jnp.concatenate(groups, axis=0).astype(bf16)

    pl.semaphore_wait(barrier, len(near) + YS - 1 + XS - 1)

    def remote(src, dst, send, recv, b, h):
        return pltpu.make_async_remote_copy(
            src_ref=src, dst_ref=dst, send_sem=send, recv_sem=recv,
            device_id=(b, h), device_id_type=pl.DeviceIdType.MESH,
        )

    row = gathered.at[pl.ds(mine, 1)]
    first = [
        remote(row, row, s1.at[i], r1.at[i], board_of(x, y, (core + dc) % CS), (hand + dz) % ZS)
        for i, (dz, dc) in enumerate(near)
    ]
    for c in first:
        c.start()
    build(0, 2)
    for c in first:
        c.wait_recv()
    group = gathered.at[pl.ds((x * YS + y) * 8, 8)]
    second = [
        remote(group, group, s2.at[k - 1], r2.at[k - 1], board_of(x, (y + k) % YS, core), hand)
        for k in range(1, YS)
    ]
    for c in second:
        c.start()
    build(2, 4)
    for c in second:
        c.wait_recv()
    plane = gathered.at[pl.ds(x * 32, 32)]
    third = [
        remote(plane, plane, s3.at[k - 1], r3.at[k - 1], board_of((x + k) % XS, y, core), hand)
        for k in range(1, XS)
    ]
    for c in third:
        c.start()
    build(4, 6)
    loads[6].wait()
    for c in third:
        c.wait_recv()

    every = gathered[:, 0, :]
    entry = lax.broadcasted_iota(jnp.int32, (128, 128), 0) * CHUNK + lax.broadcasted_iota(jnp.int32, (128, 128), 1)
    lane = lax.broadcasted_iota(jnp.int32, (128, 128), 1)
    every = jnp.where(lane < CHUNK, every, 0.0)
    total = jnp.sum(jnp.where(entry < HANDS, every, 0.0))
    quarter = every[0:32]
    for z in range(1, ZS):
        quarter = jnp.where(hand == z, every[32 * z : 32 * (z + 1)], quarter)
    stacked = jnp.concatenate([p.astype(f32) for p in pieces(quarter)], axis=0).astype(bf16)
    hand_at = lax.broadcasted_iota(jnp.int32, (128, OPAD), 1)
    spot = (hand_at - (hand_at // CHUNK) * CHUNK) == lax.broadcasted_iota(jnp.int32, (128, OPAD), 0)
    laid = jnp.dot(stacked, spot.astype(f32).astype(bf16), preferred_element_type=f32)
    laid = laid[0:32] + laid[32:64] + laid[64:96]
    owner = lax.broadcasted_iota(jnp.int32, (32, OPAD), 1) // CHUNK
    laid = jnp.where(owner == lax.broadcasted_iota(jnp.int32, (32, OPAD), 0), laid, 0.0)
    share = (jnp.sum(laid, axis=0, keepdims=True) / total)[:, 0:OWN]

    lines = (strat[...].reshape(NF * LINES, OWN).astype(f32) * share).astype(bf16)
    summed = jnp.dot(sel[...], lines, preferred_element_type=f32)
    wslot[pl.ds(hand, 1), :, 0:OWN] = (summed[0:24] + summed[24:48] + summed[48:72])[None]
    held = wslot.at[pl.ds(hand, 1)]
    fourth = [
        remote(held, held, s4.at[k - 1], r4.at[k - 1], board, (hand + k) % ZS) for k in range(1, ZS)
    ]
    for c in fourth:
        c.start()
    build(6, 8)
    for c in fourth:
        c.wait_recv()

    for z in range(ZS):
        wall[:, OWN * z : OWN * (z + 1)] = wslot[z, :, 0:OWN]
    cut = [p.astype(f32) for p in pieces(wall[...])]
    flop_of_lane = lax.broadcasted_iota(jnp.int32, (NF, HPAD), 0)
    values = jnp.zeros((OWN, RPAD), f32)
    for f in range(NF):
        groups = [
            jnp.where(flop_of_lane == f, cut[p][NF * a : NF * (a + 1)], 0.0)
            for p in range(PARTS) for a in range(ACTS)
        ] + [jnp.zeros((NF, HPAD), f32)]
        right = jnp.concatenate(groups, axis=0).astype(bf16)
        values += lax.dot_general(
            mat[:, HPAD * f : HPAD * (f + 1)], right, (((1,), (1,)), ((), ())), preferred_element_type=f32
        )
    values = jnp.concatenate([values, jnp.zeros((OWN, 128 - RPAD), f32)], axis=1)
    values = jnp.concatenate([values, jnp.zeros((OPAD - OWN, 128), f32)], axis=0).T
    best = None
    for a in range(ACTS):
        acted = sum(values[(p * ACTS + a) * NF : (p * ACTS + a + 1) * NF] for p in range(PARTS))
        best = acted if best is None else jnp.maximum(best, acted)
    flop_id = lax.broadcasted_iota(jnp.int32, (NF, OPAD), 0)
    scale = jnp.zeros((NF, OPAD), f32)
    weight = jnp.float32(0)
    for f in range(NF):
        iso = iso_smem[f].astype(f32)
        weight += iso
        scale = jnp.where(flop_id == f, iso / live_smem[f].astype(f32), scale)
    partial = jnp.sum(best * scale, axis=0, keepdims=True)
    partial = jnp.where(lax.broadcasted_iota(jnp.int32, (1, OPAD), 1) == OWN, weight, partial)
    final[pl.ds(board, 1)] = partial[None]
    ours = final.at[pl.ds(board, 1)]
    fifth = [
        remote(ours, ours, s5.at[k - 1], r5.at[k - 1], (board + k) % NB, hand) for k in range(1, NB)
    ]
    for c in fifth:
        c.start()
    for c in fifth:
        c.wait_recv()
    whole = jnp.sum(final[...], axis=0)
    out_ref[...] = whole[:, 0:OWN] / whole[:, OWN : OWN + 1]
    for c in first + second + third + fourth + fifth:
        c.wait_send()


def body(reach_pre, strategy, ranks, boards, river_live, iso_weight, pot, line_act):
    anywhere = pl.BlockSpec(memory_space=pl.ANY)
    smem = pl.BlockSpec(memory_space=pltpu.SMEM)
    dma = pltpu.SemaphoreType.DMA
    out = pl.pallas_call(
        kernel,
        out_shape=jax.ShapeDtypeStruct((1, OWN), f32),
        in_specs=[anywhere] * 7 + [smem] * 2,
        out_specs=pl.BlockSpec(memory_space=pltpu.VMEM),
        scratch_shapes=[
            pltpu.VMEM((CHUNK,), f32),
            pltpu.VMEM((NF, LINES, OWN), bf16),
            pltpu.VMEM((NF, RIV, HPAD), jnp.int32),
            pltpu.VMEM((NF, RIV, 5), jnp.int32),
            pltpu.VMEM((LINES,), f32),
            pltpu.VMEM((LINES,), jnp.int32),
            pltpu.VMEM((8, HPAD), f32),
            pltpu.VMEM((80, HPAD), f32),
            pltpu.VMEM((74, 16, HPAD), bf16),
            pltpu.VMEM((74, OWN, 128), bf16),
            pltpu.VMEM((8, 128), f32),
            pltpu.VMEM((OWN, HPAD), bf16),
            pltpu.VMEM((OWN, NF * HPAD), bf16),
            pltpu.VMEM((RPAD, NF * LINES), bf16),
            pltpu.VMEM((8, 128), f32),
            pltpu.VMEM((ZS, 24, OPAD), f32),
            pltpu.VMEM((24, HPAD), f32),
            pltpu.VMEM((8, 128), f32),
            pltpu.VMEM((128, 1, 128), f32),
            pltpu.VMEM((NB, 1, OPAD), f32),
            dma((7,)), dma((7,)), dma((7,)), dma((3,)), dma((3,)), dma((3,)), dma((3,)),
            dma((3,)), dma((3,)), dma((NB - 1,)), dma((NB - 1,)),
        ],
        compiler_params=pltpu.CompilerParams(collective_id=0, has_side_effects=True, vmem_limit_bytes=60 << 20),
    )(reach_pre, strategy, ranks, boards, pot, line_act, jnp.asarray(card_rows()), river_live, iso_weight)
    return out.reshape(OWN)


def solution(mesh):
    in_specs = (
        P(("board", "hand")),
        P("board", None, "hand"),
        P("board", None, None),
        P("board", None, None),
        P("board"),
        P("board"),
        P(),
        P(),
    )
    return jax.shard_map(body, mesh=mesh, in_specs=in_specs, out_specs=P("hand"), check_vma=False)
```

time: 373 us -> 42.4 us (0.11); the launches traced: 367 us -> 42.1 us
  blocking collectives: 132 us -> 0 us
  loops' own time: 62.2 us -> 0 us
  matrix products: 57.1 us -> 0 us
  local copies, waits for them, and re-layouts: 50.9 us -> 3.7 us
  Pallas kernels: 0 us -> 37.1 us
  waiting for transfers between devices: 33.1 us -> 0 us
  other arithmetic: 18.5 us -> 1.25 us
  between operations: 13.5 us -> 0.01 us
    unnamed x1 -> x0, blocking collectives: 68.7 us -> none
    psum x1 -> x0, blocking collectives: 63.4 us -> none  [body(): summed = lax.psum(partial_values, 'board')]
    another operation x9 -> x0, loops' own time: 62.2 us -> none  [the longest x8 45.6 us: runout_sum(): return lax.fori_loop(0, ranks_flop.shape[0], every_step, empty)]
    dot_general x65 -> x0, matrix products: 57.1 us -> none  [the longest x64 56 us: add_runout(): lax.dot_general(matrix, reach_flop, (((1,), (1,)), ((), ())), preferred_e...]
    pallas_call x0 -> x1, Pallas kernels: none -> 37.1 us  [body(): pl.pallas_call(kernel, out_shape=jax.ShapeDtypeStruct((1, OWN), f32), in_...]
    all_gather x1 -> x0, waiting for transfers between devices: 33.1 us -> none  [body(): every_reach = lax.all_gather(line_reach, 'hand', axis=2, tiled=True)]
    dynamic_slice x227 -> x0, local copies, waits for them, and re-layouts: 30 us -> none  [the longest x16 6.53 us: own_rows(): boards[flop_index]]
    squeeze x16 -> x0, local copies, waits for them, and re-layouts: 14.5 us -> none  [the longest x8 8.15 us: own_rows(): every_reach[flop_index]]
  transfers between devices with their start and end apart: 1 -> 0, of which waited for: 1 -> 0; matrix products, arithmetic and copies ran while one was open for 0% -> 0% of each run, Pallas kernels for 0% -> 0%
where the time goes in v1:
time: 42.4 us; the launch traced here: 42.1 us
  Pallas kernels  37.1 us (88%)
  local copies, waits for them, and re-layouts  3.7 us (9%)
  other arithmetic  1.25 us (3%)
    pallas_call x1, Pallas kernels, body(): pl.pallas_call(kernel, out_shape=jax.ShapeDtypeStruct((1, OWN), f32), in_...  37.1 us
    unnamed x2, local copies, waits for them, and re-layouts  3.7 us
    pallas_call x1, other arithmetic, body(): pl.pallas_call(kernel, out_shape=jax.ShapeDtypeStruct((1, OWN), f32), in_...  1.25 us

profile of v1, /device:TPU:1, one launch (start us, length us, event | category | flops | bytes accessed | tf_op | source)
XLA Modules:
  0.0 42.1 jit_solution(9735716982663672368)
XLA Ops:
  0.0 1.4 %copy.11.boards_hbm = s32[8,8,5]{2,1,0:T(8,128)} copy(s32[8,8,5]{1,0,2:T(8,128)} %param.12) | data formatting | bytes 2560 | tf_op args[3]
  1.4 2.3 %copy.10.strategy_hbm = bf16[8,128,352]{2,1,0:T(8,128)(2,1)} copy(bf16[8,128,352]{1,2,0:T(8,128)(2,1)} %param.10) | data formatting | bytes 1441792 | tf_op args[1]
  3.7 37.1 %shard_map.91 = f32[1,352]{1,0:T(1,128)} custom-call(f32[11]{0:T(128)} %reach_hbm.1, bf16[8,128,352]{2,1,0:T(8,128)(2,1)} %copy.10.strategy_hbm, s32[8,8,1408]{2,1,0:T(8,128)} %ranks_hbm.1, s32[8,8,5]{2,1,0:T(8,128)} %copy.11.boards_hbm, f32[128]{0:T(128)} %pot_hbm.1, s32[128]{0:T(128)} %act_hbm.1, f32[8,1408]{1,0:T(8,128)} %constant.2.clone.cards_hbm, ...), custom_call_target="tpu_custom_call" | custom-call | tf_op jit(solution)/shard_map/pallas_call | solution.py:274
  40.9 1.3 %reduce = f32[352]{0:T(512)} reduce(f32[1,352]{1,0:T(1,128)} %shard_map.91, f32[]{:T(128)} %constant.9), dimensions={0}, to_apply=%pallas_call.3.reduce_sub_computation | reduce | bytes 2820 | tf_op jit(solution)/shard_map/pallas_call | solution.py:274

commit v2 on v1

v2 whole, which is shorter than its diff:
```python
import functools

import jax
import jax.numpy as jnp
import numpy as np
from jax import lax
from jax.experimental import pallas as pl
from jax.experimental.pallas import tpu as pltpu
from jax.sharding import PartitionSpec as P

HANDS = 1326
HPAD = 1408
RIV = 8
LINES = 128
ACTS = 3
NF = 8
OWN = 352
OPAD = 384
CHUNK = 11
DEAD = 128.0
ZS, NB = 4, 32
PARTS = 3
ROWS = PARTS * ACTS * NF
RPAD = 80
WIDE = 256
SPLIT = (3, 5)
f32, bf16 = jnp.float32, jnp.bfloat16


def card_rows():
    first, second = np.triu_indices(52, 1)
    padding = HPAD - HANDS
    rows = np.zeros((8, HPAD), np.float32)
    rows[0] = np.concatenate([first, np.full(padding, 52)])
    rows[1] = np.concatenate([second, np.full(padding, 53)])
    rows[2] = np.arange(HPAD) < HANDS
    return rows


def pieces(value):
    high = value.astype(bf16)
    rest = value - high.astype(f32)
    middle = rest.astype(bf16)
    low = (rest - middle.astype(f32)).astype(bf16)
    return high, middle, low


def kernel(
    reach_hbm, strategy_hbm, ranks_hbm, boards_hbm, pot_hbm, act_hbm, cards_hbm, live_hbm, iso_hbm,
    out_ref,
    reach_in, strat, ranks, boards, pot, act, cards, live_smem, iso_smem,
    rk, rows_b, cols_b, block, mat, sel, spots, wslot, wall, gathered, final,
    load_sem, s1, r1, s2, r2, s4, r4, s5, r5,
):
    board, hand = lax.axis_index("board"), lax.axis_index("hand")

    reach_load = pltpu.make_async_copy(reach_hbm, reach_in, load_sem.at[0])
    reach_load.start()
    barrier = pltpu.get_barrier_semaphore()

    def greet(b, h):
        pl.semaphore_signal(barrier, inc=1, device_id=(b, h), device_id_type=pl.DeviceIdType.MESH)

    for k in range(1, NB):
        greet((board + k) % NB, hand)
    for k in range(1, ZS):
        greet(board, (hand + k) % ZS)

    loads = [
        pltpu.make_async_copy(a, b, load_sem.at[i + 1])
        for i, (a, b) in enumerate(
            [(cards_hbm, cards), (boards_hbm, boards), (live_hbm, live_smem), (iso_hbm, iso_smem),
             (ranks_hbm, ranks), (pot_hbm, pot), (act_hbm, act), (strategy_hbm, strat)]
        )
    ]
    for c in loads:
        c.start()
    reach_load.wait()
    gathered[pl.ds(hand, 1), pl.ds(board, 1), 0:1, 0:CHUNK] = reach_in[...].reshape(1, 1, 1, CHUNK)

    def remote(src, dst, send, recv, b, h):
        return pltpu.make_async_remote_copy(
            src_ref=src, dst_ref=dst, send_sem=send, recv_sem=recv,
            device_id=(b, h), device_id_type=pl.DeviceIdType.MESH,
        )

    pl.semaphore_wait(barrier, NB - 1 + ZS - 1)
    row = gathered.at[hand, pl.ds(board, 1)]
    first = [
        remote(row, row, s1.at[k - 1], r1.at[k - 1], (board + k) % NB, hand) for k in range(1, NB)
    ]
    for c in first:
        c.start()
    for c in loads[:5]:
        c.wait()

    c1, c2, alive = cards[0:1, :], cards[1:2, :], cards[2:3, :]
    runout = lax.broadcasted_iota(jnp.int32, (RIV, 1), 0)
    for f in range(NF):
        dead = jnp.broadcast_to(alive < 0.5, (RIV, HPAD))
        for k in range(5):
            card = boards[k, f].astype(f32).reshape(1, RIV)
            card = jnp.broadcast_to(card, (RIV, RIV))
            diagonal = lax.broadcasted_iota(jnp.int32, (RIV, RIV), 0) == lax.broadcasted_iota(jnp.int32, (RIV, RIV), 1)
            card = jnp.sum(jnp.where(diagonal, card, 0.0), axis=1, keepdims=True)
            dead = dead | (c1 == card) | (c2 == card)
        dead = dead | (runout >= live_smem[f])
        here = jnp.where(dead, DEAD, ranks[f].astype(f32))
        rk[RIV * f : RIV * (f + 1), :] = here
        rk[64 + f : 65 + f, :] = jnp.sum(dead.astype(f32), axis=0, keepdims=True)
    rk[72:74, :] = cards[0:2, :]
    rk[74:80, :] = jnp.zeros((6, HPAD), f32)

    own = rk[:, 0:OPAD]
    for z in range(1, ZS):
        if z < ZS - 1:
            part = rk[:, OWN * z : OWN * z + OPAD]
        else:
            part = jnp.concatenate([rk[:, OWN * z :], jnp.zeros((80, OPAD - OWN), f32)], axis=1)
        own = jnp.where(hand == z, part, own)
    own = jnp.concatenate([own, jnp.zeros((48, OPAD), f32)], axis=0)
    columns = own.T[0:OWN, :]
    for q in range(74):
        cols_b[q] = jnp.broadcast_to(columns[:, q : q + 1], (OWN, WIDE)).astype(bf16)
    for q in range(74):
        rows_b[q] = jnp.broadcast_to(rk[q : q + 1, :], (8, HPAD)).astype(bf16)

    one = jnp.ones((), bf16)

    def spread(row):
        return jnp.broadcast_to(row[None], (OWN // 8, 8, row.shape[1])).reshape(OWN, row.shape[1])

    def block_of(at, wide):
        a1, a2 = cols_b[72, :, 0:wide], cols_b[73, :, 0:wide]
        b1, b2 = spread(rows_b[72, :, at]), spread(rows_b[73, :, at])
        product = ((a1 - b1) * (a1 - b2)) * ((a2 - b1) * (a2 - b2))
        block[:, at] = jnp.minimum(jnp.abs(product), one)

    def tile_of_block(t, carry):
        block_of(pl.ds(pl.multiple_of(t * WIDE, WIDE), WIDE), WIDE)
        return carry

    lax.fori_loop(0, HPAD // WIDE, tile_of_block, 0)
    block_of(pl.ds(HPAD // WIDE * WIDE, 128), 128)

    def build_at(f, start, wide):
        at = pl.ds(start, wide)
        acc = spread(rows_b[64 + f, :, at]) - cols_b[64 + f, :, 0:wide]
        for r in range(RIV):
            gap = cols_b[RIV * f + r, :, 0:wide] - spread(rows_b[RIV * f + r, :, at])
            acc = acc + jnp.maximum(jnp.minimum(gap, one), -one)
        mat[:, pl.ds(pl.multiple_of(f * HPAD + start, 128), wide)] = acc * block[:, at]

    def build(lo, hi):
        tiles = HPAD // WIDE

        def step(i, carry):
            build_at(i // tiles, pl.multiple_of((i % tiles) * WIDE, WIDE), WIDE)
            return carry

        def tail(f, carry):
            build_at(f, tiles * WIDE, 128)
            return carry

        lax.fori_loop(lo * tiles, hi * tiles, step, 0)
        lax.fori_loop(lo, hi, tail, 0)

    for c in loads[5:7]:
        c.wait()
    flop_of_row = lax.broadcasted_iota(jnp.int32, (NF, 128), 0)
    pot_row, act_row = pot[...].reshape(1, LINES), act[...].reshape(1, LINES)
    weights = [pieces(jnp.where(act_row == a, pot_row, 0.0)) for a in range(ACTS)]
    for f in range(NF):
        groups = [
            jnp.where(flop_of_row == f, jnp.broadcast_to(weights[a][p].astype(f32), (NF, LINES)), 0.0)
            for p in range(PARTS) for a in range(ACTS)
        ] + [jnp.zeros((NF, LINES), f32)]
        sel[f] = jnp.concatenate(groups, axis=0).astype(bf16)

    at_hand = lax.broadcasted_iota(jnp.int32, (OWN, 128), 0)
    at_lane = lax.broadcasted_iota(jnp.int32, (OWN, 128), 1)
    chunk = at_hand // CHUNK
    place = (chunk % ZS) * 8 + chunk // ZS
    spots[...] = ((at_lane % 32 == place) & (at_lane < 96)).astype(f32).astype(bf16)

    build(0, SPLIT[0])
    for c in first:
        c.wait_recv()
    plane = gathered.at[pl.ds(hand, 1)]
    second = [
        remote(plane, plane, s2.at[k - 1], r2.at[k - 1], board, (hand + k) % ZS) for k in (2, 1, 3)
    ]
    for c in second:
        c.start()
    build(SPLIT[0], SPLIT[1])
    loads[7].wait()
    for c in second:
        c.wait_recv()

    every = gathered[:, :, 0, :].reshape(128, 128)
    at_row = lax.broadcasted_iota(jnp.int32, (128, 128), 0)
    lane = lax.broadcasted_iota(jnp.int32, (128, 128), 1)
    entry = ((at_row % 32) * ZS + at_row // 32) * CHUNK + lane
    total = jnp.sum(jnp.where((lane < CHUNK) & (entry < HANDS), every, 0.0))
    quarter = jnp.concatenate([gathered[z, pl.ds(hand * 8, 8), 0, :] for z in range(ZS)], axis=0)
    stacked = jnp.concatenate([p.astype(f32) for p in pieces(quarter / total)] + [jnp.zeros((32, 128), f32)], axis=0)
    laid = jnp.dot(spots[...], stacked.astype(bf16), preferred_element_type=f32)
    share = jnp.sum(jnp.where(at_lane == at_hand - chunk * CHUNK, laid, 0.0), axis=1, keepdims=True)

    summed = jnp.zeros((RPAD, OWN), f32)
    for f in range(NF):
        lines = (strat[f].astype(f32) * share).astype(bf16)
        summed += lax.dot_general(sel[f], lines, (((1,), (1,)), ((), ())), preferred_element_type=f32)
    wslot[pl.ds(hand, 1), :, 0:OWN] = (summed[0:24] + summed[24:48] + summed[48:72])[None]
    held = wslot.at[pl.ds(hand, 1)]
    fourth = [
        remote(held, held, s4.at[k - 1], r4.at[k - 1], board, (hand + k) % ZS) for k in (2, 1, 3)
    ]
    for c in fourth:
        c.start()
    build(SPLIT[1], NF)
    for c in fourth:
        c.wait_recv()

    for z in range(ZS):
        wall[:, OWN * z : OWN * (z + 1)] = wslot[z, :, 0:OWN]
    cut = [p.astype(f32) for p in pieces(wall[...])]
    flop_of_lane = lax.broadcasted_iota(jnp.int32, (NF, HPAD), 0)
    values = jnp.zeros((OWN, RPAD), f32)
    for f in range(NF):
        groups = [
            jnp.where(flop_of_lane == f, cut[p][NF * a : NF * (a + 1)], 0.0)
            for p in range(PARTS) for a in range(ACTS)
        ] + [jnp.zeros((NF, HPAD), f32)]
        right = jnp.concatenate(groups, axis=0).astype(bf16)
        values += lax.dot_general(
            mat[:, HPAD * f : HPAD * (f + 1)], right, (((1,), (1,)), ((), ())), preferred_element_type=f32
        )
    values = jnp.concatenate([values, jnp.zeros((OWN, 128 - RPAD), f32)], axis=1)
    values = jnp.concatenate([values, jnp.zeros((OPAD - OWN, 128), f32)], axis=0).T
    best = None
    for a in range(ACTS):
        acted = sum(values[(p * ACTS + a) * NF : (p * ACTS + a + 1) * NF] for p in range(PARTS))
        best = acted if best is None else jnp.maximum(best, acted)
    flop_id = lax.broadcasted_iota(jnp.int32, (NF, OPAD), 0)
    scale = jnp.zeros((NF, OPAD), f32)
    weight = jnp.float32(0)
    for f in range(NF):
        iso = iso_smem[f].astype(f32)
        weight += iso
        scale = jnp.where(flop_id == f, iso / live_smem[f].astype(f32), scale)
    partial = jnp.sum(best * scale, axis=0, keepdims=True)
    partial = jnp.where(lax.broadcasted_iota(jnp.int32, (1, OPAD), 1) == OWN, weight, partial)
    final[pl.ds(board, 1)] = partial[None]
    ours = final.at[pl.ds(board, 1)]
    fifth = [
        remote(ours, ours, s5.at[k - 1], r5.at[k - 1], (board + k) % NB, hand) for k in range(1, NB)
    ]
    for c in fifth:
        c.start()
    for c in fifth:
        c.wait_recv()
    whole = jnp.sum(final[...], axis=0)
    out_ref[...] = (whole[:, 0:OWN] / whole[:, OWN : OWN + 1]).reshape(OWN)
    for c in first + second + fourth + fifth:
        c.wait_send()


def body(reach_pre, strategy, ranks, boards, river_live, iso_weight, pot, line_act):
    anywhere = pl.BlockSpec(memory_space=pl.ANY)
    dma = pltpu.SemaphoreType.DMA
    return pl.pallas_call(
        kernel,
        out_shape=jax.ShapeDtypeStruct((OWN,), f32),
        in_specs=[anywhere] * 9,
        out_specs=pl.BlockSpec(memory_space=pltpu.VMEM),
        scratch_shapes=[
            pltpu.VMEM((CHUNK,), f32),
            pltpu.VMEM((NF, OWN, LINES), bf16),
            pltpu.VMEM((NF, RIV, HPAD), jnp.int32),
            pltpu.VMEM((5, NF, RIV), jnp.int32),
            pltpu.VMEM((LINES,), f32),
            pltpu.VMEM((LINES,), jnp.int32),
            pltpu.VMEM((8, HPAD), f32),
            pltpu.SMEM((NF,), jnp.int32),
            pltpu.SMEM((NF,), jnp.int32),
            pltpu.VMEM((80, HPAD), f32),
            pltpu.VMEM((74, 8, HPAD), bf16),
            pltpu.VMEM((74, OWN, WIDE), bf16),
            pltpu.VMEM((OWN, HPAD), bf16),
            pltpu.VMEM((OWN, NF * HPAD), bf16),
            pltpu.VMEM((NF, RPAD, LINES), bf16),
            pltpu.VMEM((OWN, 128), bf16),
            pltpu.VMEM((ZS, 24, OPAD), f32),
            pltpu.VMEM((24, HPAD), f32),
            pltpu.VMEM((ZS, NB, 1, 128), f32),
            pltpu.VMEM((NB, 1, OPAD), f32),
            dma((9,)), dma((NB - 1,)), dma((NB - 1,)), dma((3,)), dma((3,)), dma((3,)), dma((3,)),
            dma((NB - 1,)), dma((NB - 1,)),
        ],
        compiler_params=pltpu.CompilerParams(collective_id=0, has_side_effects=True, vmem_limit_bytes=60 << 20),
    )(
        reach_pre, jnp.swapaxes(strategy, 1, 2), ranks, jnp.transpose(boards, (2, 0, 1)),
        pot, line_act, jnp.asarray(card_rows()), river_live, iso_weight,
    )


def solution(mesh):
    in_specs = (
        P(("board", "hand")),
        P("board", None, "hand"),
        P("board", None, None),
        P("board", None, None),
        P("board"),
        P("board"),
        P(),
        P(),
    )
    return jax.shard_map(body, mesh=mesh, in_specs=in_specs, out_specs=P("hand"), check_vma=False)
```

time: 42.4 us -> 33.9 us (0.80)
  Pallas kernels: 37.1 us -> 32.5 us
  local copies, waits for them, and re-layouts: 3.7 us -> 1.26 us
  other arithmetic: 1.25 us -> 0 us
    pallas_call x1, Pallas kernels: 37.1 us -> 32.5 us  [body(): pl.pallas_call(kernel, out_shape=jax.ShapeDtypeStruct((OWN,), f32), in_sp...]
    unnamed x2 -> x1, local copies, waits for them, and re-layouts: 3.7 us -> 1.26 us
    pallas_call x1 -> x0, other arithmetic: 1.25 us -> none  [body(): pl.pallas_call(kernel, out_shape=jax.ShapeDtypeStruct((1, OWN), f32), in_...]
where the time goes in v2:
time: 33.9 us; the launch traced here: 33.8 us
  Pallas kernels  32.5 us (96%)
  local copies, waits for them, and re-layouts  1.26 us (4%)
    pallas_call x1, Pallas kernels, body(): pl.pallas_call(kernel, out_shape=jax.ShapeDtypeStruct((OWN,), f32), in_sp...  32.5 us
    unnamed x1, local copies, waits for them, and re-layouts  1.26 us

profile of v2, /device:TPU:1, one launch (start us, length us, event | category | flops | bytes accessed | tf_op | source)
XLA Modules:
  0.0 33.8 jit_solution(16817087359192678530)
XLA Ops:
  0.0 32.5 %shard_map.91 = f32[352]{0:T(512)} custom-call(f32[11]{0:T(128)} %reach_hbm.1, bf16[8,352,128]{2,1,0:T(8,128)(2,1)} %bitcast.2, s32[8,8,1408]{2,1,0:T(8,128)} %ranks_hbm.1, s32[5,8,8]{2,1,0:T(8,128)} %bitcast.3, f32[128]{0:T(128)} %pot_hbm.1, s32[128]{0:T(128)} %act_hbm.1, f32[8,1408]{1,0:T(8,128)} %constant.2.clone.cards_hbm, s32[8]{0:T(128)} %live_hbm.1, ...), custom_call_target="tpu_custom_call" | custom-call | tf_op jit(solution)/shard_map/pallas_call | solution.py:272
  32.5 1.3 %copy.11 = f32[352]{0:T(512)} copy(f32[352]{0:T(512)} %shard_map.91) | data formatting | bytes 2816

commit v3 on v2

v3 whole, which is shorter than its diff:
```python
import functools

import jax
import jax.numpy as jnp
import numpy as np
from jax import lax
from jax.experimental import pallas as pl
from jax.experimental.pallas import tpu as pltpu
from jax.sharding import PartitionSpec as P

HANDS = 1326
HPAD = 1408
RIV = 8
LINES = 128
ACTS = 3
NF = 8
OWN = 352
OPAD = 384
CHUNK = 11
DEAD = 128.0
ZS, NB = 4, 32
PARTS = 3
ROWS = PARTS * ACTS * NF
RPAD = 80
HALF = NF // 2
KPAD = ZS * OPAD
STEP = 128
TOP = 96
SPLIT = (3, 6)
f32, bf16, f8 = jnp.float32, jnp.bfloat16, jnp.float8_e4m3fn


def card_rows():
    first, second = np.triu_indices(52, 1)
    padding = HPAD - HANDS
    rows = np.zeros((ZS, 8, OPAD), np.float32)
    rows[:, 0], rows[:, 1] = 52, 53
    rows[:, 0, :OWN] = np.concatenate([first, np.full(padding, 52)]).reshape(ZS, OWN)
    rows[:, 1, :OWN] = np.concatenate([second, np.full(padding, 53)]).reshape(ZS, OWN)
    rows[:, 2, :OWN] = (np.arange(HPAD) < HANDS).reshape(ZS, OWN)
    return rows


def pieces(value):
    high = value.astype(bf16)
    rest = value - high.astype(f32)
    middle = rest.astype(bf16)
    low = (rest - middle.astype(f32)).astype(bf16)
    return high, middle, low


def kernel(
    reach_hbm, strategy_hbm, ranks_hbm, boards_hbm, pot_hbm, act_hbm, cards_hbm, live_hbm, iso_hbm,
    out_ref,
    reach_in, strat, ranks, boards, pot, act, cards, live_smem, iso_smem,
    quarters, rel, inc, lhs, slots, onehot, block, mat, sel, spots, scales, wslot, sums, gathered, final,
    load_sem, s1, r1, s2, r2, s4, r4, s5, r5,
):
    board, hand = lax.axis_index("board"), lax.axis_index("hand")
    plane_ids = [(board + k) % NB for k in range(1, NB)]

    reach_load = pltpu.make_async_copy(reach_hbm, reach_in, load_sem.at[0])
    reach_load.start()
    barrier = pltpu.get_barrier_semaphore()

    def greet(b, h):
        pl.semaphore_signal(barrier, inc=1, device_id=(b, h), device_id_type=pl.DeviceIdType.MESH)

    for b in plane_ids:
        greet(b, hand)
    for k in (2, 1, 3):
        greet(board, (hand + k) % ZS)

    loads = [
        pltpu.make_async_copy(a, b, load_sem.at[i + 1])
        for i, (a, b) in enumerate(
            [(cards_hbm, cards), (boards_hbm, boards), (live_hbm, live_smem), (iso_hbm, iso_smem),
             (ranks_hbm, ranks), (pot_hbm, pot), (act_hbm, act), (strategy_hbm, strat)]
        )
    ]
    for c in loads:
        c.start()
    reach_load.wait()
    gathered[pl.ds(hand, 1), pl.ds(board, 1), 0:1, 0:CHUNK] = reach_in[...].reshape(1, 1, 1, CHUNK)

    def remote(src, dst, send, recv, b, h):
        return pltpu.make_async_remote_copy(
            src_ref=src, dst_ref=dst, send_sem=send, recv_sem=recv,
            device_id=(b, h), device_id_type=pl.DeviceIdType.MESH,
        )

    pl.semaphore_wait(barrier, NB - 1 + ZS - 1)
    row = gathered.at[hand, pl.ds(board, 1)]
    first = [remote(row, row, s1.at[i], r1.at[i], b, hand) for i, b in enumerate(plane_ids)]
    for c in first:
        c.start()
    for c in loads[:5]:
        c.wait()

    runout = lax.broadcasted_iota(jnp.int32, (RIV, 1), 0)
    diagonal = lax.broadcasted_iota(jnp.int32, (RIV, RIV), 0) == lax.broadcasted_iota(jnp.int32, (RIV, RIV), 1)
    for f in range(NF):
        drawn = []
        for k in range(5):
            card = jnp.broadcast_to(boards[k, f].astype(f32).reshape(1, RIV), (RIV, RIV))
            drawn.append(jnp.sum(jnp.where(diagonal, card, 0.0), axis=1, keepdims=True))
        beyond = runout >= live_smem[f]
        for z in range(ZS):
            if z < ZS - 1:
                part = ranks[f, :, OWN * z : OWN * z + OPAD].astype(f32)
            else:
                part = jnp.concatenate([ranks[f, :, OWN * z :].astype(f32), jnp.zeros((RIV, OPAD - OWN), f32)], axis=1)
            dead = (cards[z, 2:3, :] < 0.5) | beyond
            for card in drawn:
                dead = dead | (cards[z, 0:1, :] == card) | (cards[z, 1:2, :] == card)
            quarters[z, RIV * f : RIV * (f + 1), :] = jnp.where(dead, DEAD, part)
    card_id = lax.broadcasted_iota(jnp.int32, (128, OPAD), 0).astype(f32)
    for z in range(ZS):
        inc[z] = ((card_id == cards[z, 0:1, :]) | (card_id == cards[z, 1:2, :])).astype(f32)

    for k in range(ZS):
        rel[:, OPAD * k : OPAD * (k + 1)] = quarters[(hand + ZS - k) % ZS]
    own = quarters[hand]
    alive = (own < DEAD).astype(f32)
    ranked = own * alive
    both = [t for f in range(NF) for t in (ranked[RIV * f : RIV * (f + 1)], alive[RIV * f : RIV * (f + 1)])]
    lhs[...] = jnp.concatenate(both, axis=0).T[0:OWN].astype(bf16)
    held_cards = inc[hand].T[0:OWN].astype(bf16)
    for k in range(ZS):
        shared = jnp.dot(held_cards, inc[(hand + ZS - k) % ZS].astype(bf16), preferred_element_type=f32)
        block[:, OPAD * k : OPAD * (k + 1)] = jnp.where(shared > 0.5, 0.0, 1.0).astype(bf16)

    slots[...] = jnp.zeros(slots.shape, bf16)
    at = lax.broadcasted_iota(jnp.int32, (2 * RIV, RIV * STEP), 1)
    which = lax.broadcasted_iota(jnp.int32, (2 * RIV, RIV * STEP), 0)
    pattern = jnp.where(which < RIV, 1.0, -(at % STEP).astype(f32))
    slots[112:128, :] = jnp.where(at // STEP == which % RIV, pattern, 0.0).astype(bf16)
    for r in range(RIV):
        onehot[STEP * r + TOP : STEP * (r + 1), :] = jnp.zeros((STEP - TOP, KPAD), bf16).astype(f8)
    slot = lax.broadcasted_iota(jnp.int32, (TOP, KPAD), 0).astype(f32).astype(bf16)
    one, zero = jnp.ones((), bf16), jnp.zeros((), bf16)

    def build(lo, hi):
        def step(f, carry):
            pick = slots[pl.ds(pl.multiple_of(112 - 16 * f, 16), 128), :]
            beats = jnp.dot(lhs[...], pick, preferred_element_type=f32)
            beats = jnp.maximum(jnp.minimum(beats, 1.0), -1.0).astype(bf16).astype(f8)
            for r in range(RIV):
                ranked = jnp.broadcast_to(rel[pl.ds(RIV * f + r, 1), :], (TOP, KPAD)).astype(bf16)
                onehot[STEP * r : STEP * r + TOP, :] = jnp.where(slot == ranked, one, zero).astype(f8)
            net = jnp.dot(beats, onehot[...], preferred_element_type=f32)
            for k in range(ZS):
                here = net[:, OPAD * k : OPAD * (k + 1)].astype(bf16) * block[:, OPAD * k : OPAD * (k + 1)]
                start = ((f // HALF) * ZS + k) * HALF * OPAD + (f % HALF) * OPAD
                mat[:, pl.ds(pl.multiple_of(start, 128), OPAD)] = here
            return carry

        lax.fori_loop(lo, hi, step, 0)

    for c in loads[5:7]:
        c.wait()
    lines_row = lax.broadcasted_iota(jnp.int32, (HALF, LINES), 0)
    pot_row, act_row = pot[...].reshape(1, LINES), act[...].reshape(1, LINES)
    weights = [pieces(jnp.where(act_row == a, pot_row, 0.0)) for a in range(ACTS)]
    for f in range(HALF):
        groups = [
            jnp.where(lines_row == f, jnp.broadcast_to(weights[a][p].astype(f32), (HALF, LINES)), 0.0)
            for p in range(PARTS) for a in range(ACTS)
        ] + [jnp.zeros((HALF, LINES), f32)]
        sel[f] = jnp.concatenate(groups, axis=0).astype(bf16)

    flop_id = lax.broadcasted_iota(jnp.int32, (NF, OPAD), 0)
    scale = jnp.zeros((NF, OPAD), f32)
    weight = jnp.float32(0)
    for f in range(NF):
        iso = iso_smem[f].astype(f32)
        weight += iso
        scale = jnp.where(flop_id == f, iso / live_smem[f].astype(f32), scale)
    scales[0] = scale
    scales[1] = jnp.full((NF, OPAD), weight)

    at_hand = lax.broadcasted_iota(jnp.int32, (OWN, 128), 0)
    at_lane = lax.broadcasted_iota(jnp.int32, (OWN, 128), 1)
    chunk = at_hand // CHUNK
    place = (chunk % ZS) * 8 + chunk // ZS
    spots[...] = ((at_lane % 32 == place) & (at_lane < 96)).astype(f32).astype(bf16)

    build(0, SPLIT[0])
    for c in first:
        c.wait_recv()
    plane = gathered.at[pl.ds(hand, 1)]
    second = [
        remote(plane, plane, s2.at[k - 1], r2.at[k - 1], board, (hand + k) % ZS) for k in (2, 1, 3)
    ]
    for c in second:
        c.start()
    build(SPLIT[0], SPLIT[1])
    loads[7].wait()
    for c in second:
        c.wait_recv()

    every = gathered[:, :, 0, :].reshape(128, 128)
    at_row = lax.broadcasted_iota(jnp.int32, (128, 128), 0)
    lane = lax.broadcasted_iota(jnp.int32, (128, 128), 1)
    entry = ((at_row % 32) * ZS + at_row // 32) * CHUNK + lane
    total = jnp.sum(jnp.where((lane < CHUNK) & (entry < HANDS), every, 0.0))
    quarter = jnp.concatenate([gathered[z, pl.ds(hand * 8, 8), 0, :] for z in range(ZS)], axis=0)
    stacked = jnp.concatenate([p.astype(f32) for p in pieces(quarter / total)] + [jnp.zeros((32, 128), f32)], axis=0)
    laid = jnp.dot(spots[...], stacked.astype(bf16), preferred_element_type=f32)
    share = jnp.sum(jnp.where(at_lane == at_hand - chunk * CHUNK, laid, 0.0), axis=1, keepdims=True)

    sent = []
    for h in range(2):
        summed = jnp.zeros((40, OWN), f32)
        for f in range(HALF):
            lines = (strat[HALF * h + f].astype(f32) * share).astype(bf16)
            summed += lax.dot_general(sel[f], lines, (((1,), (1,)), ((), ())), preferred_element_type=f32)
        summed = jnp.concatenate([summed, jnp.zeros((40, OPAD - OWN), f32)], axis=1)
        wslot[pl.ds(hand, 1), h] = (summed[0:12] + summed[12:24] + summed[24:36])[None]
        held = wslot.at[pl.ds(hand, 1), h]
        sent.append([
            remote(held, held, s4.at[3 * h + k - 1], r4.at[3 * h + k - 1], board, (hand + k) % ZS) for k in (2, 1, 3)
        ])
        for c in sent[h]:
            c.start()
    build(SPLIT[1], NF)

    flop_of_lane = lax.broadcasted_iota(jnp.int32, (NF, OPAD), 0)

    def times_reach(h, k):
        cut = [p.astype(f32) for p in pieces(wslot[(hand + ZS - k) % ZS, h])]
        columns = []
        for f in range(HALF):
            groups = [
                jnp.where(flop_of_lane == HALF * h + f, cut[p][HALF * a + f : HALF * a + f + 1], 0.0)
                for p in range(PARTS) for a in range(ACTS)
            ] + [jnp.zeros((NF, OPAD), f32)]
            columns.append(jnp.concatenate(groups, axis=0).astype(bf16))
        return columns

    def product(h, ks):
        right = jnp.concatenate([c for k in ks for c in times_reach(h, k)], axis=1)
        start = (h * ZS + ks[0]) * HALF * OPAD
        left = mat[:, start : start + len(ks) * HALF * OPAD]
        return lax.dot_general(left, right, (((1,), (1,)), ((), ())), preferred_element_type=f32)

    sums[...] = product(0, (0,)) + product(1, (0,))
    for h in range(2):
        for c in sent[h]:
            c.wait_recv()
        sums[...] += product(h, (1, 2)) + product(h, (3,))
    values = sums[...]
    values = jnp.concatenate([values, jnp.zeros((OWN, 128 - RPAD), f32)], axis=1)
    values = jnp.concatenate([values, jnp.zeros((OPAD - OWN, 128), f32)], axis=0).T
    best = None
    for a in range(ACTS):
        acted = sum(values[(p * ACTS + a) * NF : (p * ACTS + a + 1) * NF] for p in range(PARTS))
        best = acted if best is None else jnp.maximum(best, acted)
    partial = jnp.sum(best * scales[0], axis=0, keepdims=True)
    partial = jnp.where(lax.broadcasted_iota(jnp.int32, (1, OPAD), 1) == OWN, scales[1, 0:1], partial)
    final[pl.ds(board, 1)] = partial[None]
    ours = final.at[pl.ds(board, 1)]
    fifth = [remote(ours, ours, s5.at[i], r5.at[i], b, hand) for i, b in enumerate(plane_ids)]
    for c in fifth:
        c.start()
    for c in fifth:
        c.wait_recv()
    whole = jnp.sum(final[...], axis=0)
    out_ref[...] = (whole[:, 0:OWN] / whole[:, OWN : OWN + 1]).reshape(OWN)
    for c in first + second + sent[0] + sent[1] + fifth:
        c.wait_send()


def body(reach_pre, strategy, ranks, boards, river_live, iso_weight, pot, line_act):
    anywhere = pl.BlockSpec(memory_space=pl.ANY)
    dma = pltpu.SemaphoreType.DMA
    return pl.pallas_call(
        kernel,
        out_shape=jax.ShapeDtypeStruct((OWN,), f32),
        in_specs=[anywhere] * 9,
        out_specs=pl.BlockSpec(memory_space=pltpu.VMEM),
        scratch_shapes=[
            pltpu.VMEM((CHUNK,), f32),
            pltpu.VMEM((NF, OWN, LINES), bf16),
            pltpu.VMEM((NF, RIV, HPAD), jnp.int32),
            pltpu.VMEM((5, NF, RIV), jnp.int32),
            pltpu.VMEM((LINES,), f32),
            pltpu.VMEM((LINES,), jnp.int32),
            pltpu.VMEM((ZS, 8, OPAD), f32),
            pltpu.SMEM((NF,), jnp.int32),
            pltpu.SMEM((NF,), jnp.int32),
            pltpu.VMEM((ZS, NF * RIV, OPAD), f32),
            pltpu.VMEM((NF * RIV, KPAD), f32),
            pltpu.VMEM((ZS, 128, OPAD), f32),
            pltpu.VMEM((OWN, 128), bf16),
            pltpu.VMEM((256, RIV * STEP), bf16),
            pltpu.VMEM((RIV * STEP, KPAD), f8),
            pltpu.VMEM((OWN, KPAD), bf16),
            pltpu.VMEM((OWN, NF * KPAD), bf16),
            pltpu.VMEM((HALF, 40, LINES), bf16),
            pltpu.VMEM((OWN, 128), bf16),
            pltpu.VMEM((2, NF, OPAD), f32),
            pltpu.VMEM((ZS, 2, ACTS * HALF, OPAD), f32),
            pltpu.VMEM((OWN, RPAD), f32),
            pltpu.VMEM((ZS, NB, 1, 128), f32),
            pltpu.VMEM((NB, 1, OPAD), f32),
            dma((9,)), dma((NB - 1,)), dma((NB - 1,)), dma((3,)), dma((3,)), dma((6,)), dma((6,)),
            dma((NB - 1,)), dma((NB - 1,)),
        ],
        compiler_params=pltpu.CompilerParams(collective_id=0, has_side_effects=True, vmem_limit_bytes=60 << 20),
    )(
        reach_pre, jnp.swapaxes(strategy, 1, 2), ranks, jnp.transpose(boards, (2, 0, 1)),
        pot, line_act, jnp.asarray(card_rows()), river_live, iso_weight,
    )


def solution(mesh):
    in_specs = (
        P(("board", "hand")),
        P("board", None, "hand"),
        P("board", None, None),
        P("board", None, None),
        P("board"),
        P("board"),
        P(),
        P(),
    )
    return jax.shard_map(body, mesh=mesh, in_specs=in_specs, out_specs=P("hand"), check_vma=False)
```

time: 33.9 us -> 32.2 us (0.950)
  Pallas kernels: 32.5 us -> 30.8 us
    pallas_call x1, Pallas kernels: 32.5 us -> 30.8 us  [body(): pl.pallas_call(kernel, out_shape=jax.ShapeDtypeStruct((OWN,), f32), in_sp...]
where the time goes in v3:
time: 32.2 us; the launch traced here: 32.1 us
  Pallas kernels  30.8 us (96%)
  local copies, waits for them, and re-layouts  1.26 us (4%)
    pallas_call x1, Pallas kernels, body(): pl.pallas_call(kernel, out_shape=jax.ShapeDtypeStruct((OWN,), f32), in_sp...  30.8 us
    unnamed x1, local copies, waits for them, and re-layouts  1.26 us

profile of v3, /device:TPU:1, one launch (start us, length us, event | category | flops | bytes accessed | tf_op | source)
XLA Modules:
  0.0 32.1 jit_solution(14754632163404470945)
XLA Ops:
  0.0 30.8 %shard_map.91 = f32[352]{0:T(512)} custom-call(f32[11]{0:T(128)} %reach_hbm.1, bf16[8,352,128]{2,1,0:T(8,128)(2,1)} %bitcast.2, s32[8,8,1408]{2,1,0:T(8,128)} %ranks_hbm.1, s32[5,8,8]{2,1,0:T(8,128)} %bitcast.3, f32[128]{0:T(128)} %pot_hbm.1, s32[128]{0:T(128)} %act_hbm.1, f32[4,8,384]{2,1,0:T(8,128)} %constant.2.clone.cards_hbm, s32[8]{0:T(128)} %live_hbm.1, ...), custom_call_target="tpu_custom_call" | custom-call | tf_op jit(solution)/shard_map/pallas_call | solution.py:277
  30.8 1.3 %copy.11 = f32[352]{0:T(512)} copy(f32[352]{0:T(512)} %shard_map.91) | data formatting | bytes 2816

commit v4 on v3

--- a/solution.py
+++ b/solution.py
@@ -53,8 +53,8 @@
     reach_hbm, strategy_hbm, ranks_hbm, boards_hbm, pot_hbm, act_hbm, cards_hbm, live_hbm, iso_hbm,
     out_ref,
     reach_in, strat, ranks, boards, pot, act, cards, live_smem, iso_smem,
-    quarters, rel, inc, lhs, slots, onehot, block, mat, sel, spots, scales, wslot, sums, gathered, final,
-    load_sem, s1, r1, s2, r2, s4, r4, s5, r5,
+    quarters, rel, inc, lhs, slots, onehot, block, mat, sel, spots, scales, wslot, sums, gathered, parts, final,
+    load_sem, s1, r1, s2, r2, s3, r3, s4, r4, s5, r5,
 ):
     board, hand = lax.axis_index("board"), lax.axis_index("hand")
     plane_ids = [(board + k) % NB for k in range(1, NB)]
@@ -188,22 +188,27 @@
     build(0, SPLIT[0])
     for c in first:
         c.wait_recv()
-    plane = gathered.at[pl.ds(hand, 1)]
-    second = [
-        remote(plane, plane, s2.at[k - 1], r2.at[k - 1], board, (hand + k) % ZS) for k in (2, 1, 3)
-    ]
+    second = []
+    for k in (2, 1, 3):
+        rows_of = gathered.at[hand, pl.ds(((hand + k) % ZS) * 8, 8)]
+        second.append(remote(rows_of, rows_of, s2.at[k - 1], r2.at[k - 1], board, (hand + k) % ZS))
     for c in second:
+        c.start()
+    plane = gathered[pl.ds(hand, 1), :, 0, :].reshape(NB, 128)
+    lane = lax.broadcasted_iota(jnp.int32, (NB, 128), 1)
+    entry = (lax.broadcasted_iota(jnp.int32, (NB, 128), 0) * ZS + hand) * CHUNK + lane
+    plane = jnp.where((lane < CHUNK) & (entry < HANDS), plane, 0.0)
+    parts[pl.ds(hand, 1)] = jnp.sum(plane, axis=0, keepdims=True)[None]
+    part = parts.at[pl.ds(hand, 1)]
+    third = [remote(part, part, s3.at[k - 1], r3.at[k - 1], board, (hand + k) % ZS) for k in (2, 1, 3)]
+    for c in third:
         c.start()
     build(SPLIT[0], SPLIT[1])
     loads[7].wait()
-    for c in second:
+    for c in second + third:
         c.wait_recv()
 
-    every = gathered[:, :, 0, :].reshape(128, 128)
-    at_row = lax.broadcasted_iota(jnp.int32, (128, 128), 0)
-    lane = lax.broadcasted_iota(jnp.int32, (128, 128), 1)
-    entry = ((at_row % 32) * ZS + at_row // 32) * CHUNK + lane
-    total = jnp.sum(jnp.where((lane < CHUNK) & (entry < HANDS), every, 0.0))
+    total = jnp.sum(jnp.sum(parts[...], axis=0))
     quarter = jnp.concatenate([gathered[z, pl.ds(hand * 8, 8), 0, :] for z in range(ZS)], axis=0)
     stacked = jnp.concatenate([p.astype(f32) for p in pieces(quarter / total)] + [jnp.zeros((32, 128), f32)], axis=0)
     laid = jnp.dot(spots[...], stacked.astype(bf16), preferred_element_type=f32)
@@ -244,11 +249,13 @@
         left = mat[:, start : start + len(ks) * HALF * OPAD]
         return lax.dot_general(left, right, (((1,), (1,)), ((), ())), preferred_element_type=f32)
 
-    sums[...] = product(0, (0,)) + product(1, (0,))
+    sums[...] = jnp.zeros((OWN, RPAD), f32)
+    sums[...] += product(0, (0,))
+    sums[...] += product(1, (0,))
     for h in range(2):
         for c in sent[h]:
             c.wait_recv()
-        sums[...] += product(h, (1, 2)) + product(h, (3,))
+        sums[...] += product(h, (1, 2, 3))
     values = sums[...]
     values = jnp.concatenate([values, jnp.zeros((OWN, 128 - RPAD), f32)], axis=1)
     values = jnp.concatenate([values, jnp.zeros((OPAD - OWN, 128), f32)], axis=0).T
@@ -267,7 +274,7 @@
         c.wait_recv()
     whole = jnp.sum(final[...], axis=0)
     out_ref[...] = (whole[:, 0:OWN] / whole[:, OWN : OWN + 1]).reshape(OWN)
-    for c in first + second + sent[0] + sent[1] + fifth:
+    for c in first + second + third + sent[0] + sent[1] + fifth:
         c.wait_send()
 
 
@@ -303,8 +310,9 @@
             pltpu.VMEM((ZS, 2, ACTS * HALF, OPAD), f32),
             pltpu.VMEM((OWN, RPAD), f32),
             pltpu.VMEM((ZS, NB, 1, 128), f32),
+            pltpu.VMEM((ZS, 1, 128), f32),
             pltpu.VMEM((NB, 1, OPAD), f32),
-            dma((9,)), dma((NB - 1,)), dma((NB - 1,)), dma((3,)), dma((3,)), dma((6,)), dma((6,)),
+            dma((9,)), dma((NB - 1,)), dma((NB - 1,)), dma((3,)), dma((3,)), dma((3,)), dma((3,)), dma((6,)), dma((6,)),
             dma((NB - 1,)), dma((NB - 1,)),
         ],
         compiler_params=pltpu.CompilerParams(collective_id=0, has_side_effects=True, vmem_limit_bytes=60 << 20),

time: 32.2 us -> 31.5 us (0.978)
  Pallas kernels: 30.8 us -> 30.1 us
    pallas_call x1, Pallas kernels: 30.8 us -> 30.1 us  [body(): pl.pallas_call(kernel, out_shape=jax.ShapeDtypeStruct((OWN,), f32), in_sp...]
where the time goes in v4:
time: 31.5 us; the launch traced here: 31.3 us
  Pallas kernels  30.1 us (96%)
  local copies, waits for them, and re-layouts  1.26 us (4%)
    pallas_call x1, Pallas kernels, body(): pl.pallas_call(kernel, out_shape=jax.ShapeDtypeStruct((OWN,), f32), in_sp...  30.1 us
    unnamed x1, local copies, waits for them, and re-layouts  1.26 us

profile of v4, /device:TPU:1, one launch (start us, length us, event | category | flops | bytes accessed | tf_op | source)
XLA Modules:
  0.0 31.3 jit_solution(234457476563405670)
XLA Ops:
  0.0 30.1 %shard_map.91 = f32[352]{0:T(512)} custom-call(f32[11]{0:T(128)} %reach_hbm.1, bf16[8,352,128]{2,1,0:T(8,128)(2,1)} %bitcast.2, s32[8,8,1408]{2,1,0:T(8,128)} %ranks_hbm.1, s32[5,8,8]{2,1,0:T(8,128)} %bitcast.3, f32[128]{0:T(128)} %pot_hbm.1, s32[128]{0:T(128)} %act_hbm.1, f32[4,8,384]{2,1,0:T(8,128)} %constant.2.clone.cards_hbm, s32[8]{0:T(128)} %live_hbm.1, ...), custom_call_target="tpu_custom_call" | custom-call | tf_op jit(solution)/shard_map/pallas_call | solution.py:284
  30.1 1.3 %copy.11 = f32[352]{0:T(512)} copy(f32[352]{0:T(512)} %shard_map.91) | data formatting | bytes 2816

commit v5 on v4

--- a/solution.py
+++ b/solution.py
@@ -221,7 +221,9 @@
             lines = (strat[HALF * h + f].astype(f32) * share).astype(bf16)
             summed += lax.dot_general(sel[f], lines, (((1,), (1,)), ((), ())), preferred_element_type=f32)
         summed = jnp.concatenate([summed, jnp.zeros((40, OPAD - OWN), f32)], axis=1)
-        wslot[pl.ds(hand, 1), h] = (summed[0:12] + summed[12:24] + summed[24:36])[None]
+        acts = summed[0:12] + summed[12:24] + summed[24:36]
+        for a in range(ACTS):
+            wslot[pl.ds(hand, 1), h, a] = acts[HALF * a : HALF * (a + 1)][None]
         held = wslot.at[pl.ds(hand, 1), h]
         sent.append([
             remote(held, held, s4.at[3 * h + k - 1], r4.at[3 * h + k - 1], board, (hand + k) % ZS) for k in (2, 1, 3)
@@ -237,7 +239,7 @@
         columns = []
         for f in range(HALF):
             groups = [
-                jnp.where(flop_of_lane == HALF * h + f, cut[p][HALF * a + f : HALF * a + f + 1], 0.0)
+                jnp.where(flop_of_lane == HALF * h + f, cut[p][a, f : f + 1], 0.0)
                 for p in range(PARTS) for a in range(ACTS)
             ] + [jnp.zeros((NF, OPAD), f32)]
             columns.append(jnp.concatenate(groups, axis=0).astype(bf16))
@@ -307,7 +309,7 @@
             pltpu.VMEM((HALF, 40, LINES), bf16),
             pltpu.VMEM((OWN, 128), bf16),
             pltpu.VMEM((2, NF, OPAD), f32),
-            pltpu.VMEM((ZS, 2, ACTS * HALF, OPAD), f32),
+            pltpu.VMEM((ZS, 2, ACTS, HALF, OPAD), f32),
             pltpu.VMEM((OWN, RPAD), f32),
             pltpu.VMEM((ZS, NB, 1, 128), f32),
             pltpu.VMEM((ZS, 1, 128), f32),

time: 31.5 us -> 31.4 us (level)
  no operation moved by 1% of the time
where the time goes in v5:
time: 31.4 us; the launch traced here: 31.3 us
  Pallas kernels  30 us (96%)
  local copies, waits for them, and re-layouts  1.26 us (4%)
    pallas_call x1, Pallas kernels, body(): pl.pallas_call(kernel, out_shape=jax.ShapeDtypeStruct((OWN,), f32), in_sp...  30 us
    unnamed x1, local copies, waits for them, and re-layouts  1.26 us

profile of v5, /device:TPU:1, one launch (start us, length us, event | category | flops | bytes accessed | tf_op | source)
XLA Modules:
  0.0 31.3 jit_solution(6033144183534842347)
XLA Ops:
  0.0 30.0 %shard_map.91 = f32[352]{0:T(512)} custom-call(f32[11]{0:T(128)} %reach_hbm.1, bf16[8,352,128]{2,1,0:T(8,128)(2,1)} %bitcast.2, s32[8,8,1408]{2,1,0:T(8,128)} %ranks_hbm.1, s32[5,8,8]{2,1,0:T(8,128)} %bitcast.3, f32[128]{0:T(128)} %pot_hbm.1, s32[128]{0:T(128)} %act_hbm.1, f32[4,8,384]{2,1,0:T(8,128)} %constant.2.clone.cards_hbm, s32[8]{0:T(128)} %live_hbm.1, ...), custom_call_target="tpu_custom_call" | custom-call | tf_op jit(solution)/shard_map/pallas_call | solution.py:286
  30.0 1.3 %copy.11 = f32[352]{0:T(512)} copy(f32[352]{0:T(512)} %shard_map.91) | data formatting | bytes 2816

commit v6 on v5

--- a/solution.py
+++ b/solution.py
@@ -21,7 +21,7 @@
 ZS, NB = 4, 32
 PARTS = 3
 ROWS = PARTS * ACTS * NF
-RPAD = 80
+RPAD = 72
 HALF = NF // 2
 KPAD = ZS * OPAD
 STEP = 128
@@ -241,7 +241,7 @@
             groups = [
                 jnp.where(flop_of_lane == HALF * h + f, cut[p][a, f : f + 1], 0.0)
                 for p in range(PARTS) for a in range(ACTS)
-            ] + [jnp.zeros((NF, OPAD), f32)]
+            ]
             columns.append(jnp.concatenate(groups, axis=0).astype(bf16))
         return columns
 

time: 31.4 us -> 31.4 us (level)
  no operation moved by 1% of the time
where the time goes in v6:
time: 31.4 us; the launch traced here: 31.3 us
  Pallas kernels  30 us (96%)
  local copies, waits for them, and re-layouts  1.26 us (4%)
    pallas_call x1, Pallas kernels, body(): pl.pallas_call(kernel, out_shape=jax.ShapeDtypeStruct((OWN,), f32), in_sp...  30 us
    unnamed x1, local copies, waits for them, and re-layouts  1.26 us

profile of v6, /device:TPU:1, one launch (start us, length us, event | category | flops | bytes accessed | tf_op | source)
XLA Modules:
  0.0 31.3 jit_solution(7824919268865377122)
XLA Ops:
  0.0 30.0 %shard_map.91 = f32[352]{0:T(512)} custom-call(f32[11]{0:T(128)} %reach_hbm.1, bf16[8,352,128]{2,1,0:T(8,128)(2,1)} %bitcast.2, s32[8,8,1408]{2,1,0:T(8,128)} %ranks_hbm.1, s32[5,8,8]{2,1,0:T(8,128)} %bitcast.3, f32[128]{0:T(128)} %pot_hbm.1, s32[128]{0:T(128)} %act_hbm.1, f32[4,8,384]{2,1,0:T(8,128)} %constant.2.clone.cards_hbm, s32[8]{0:T(128)} %live_hbm.1, ...), custom_call_target="tpu_custom_call" | custom-call | tf_op jit(solution)/shard_map/pallas_call | solution.py:286
  30.0 1.3 %copy.11 = f32[352]{0:T(512)} copy(f32[352]{0:T(512)} %shard_map.91) | data formatting | bytes 2816
